TPU v7x, 128 devices: a whole 4x4x4 slice. The times are simulated.
128 devices in a mesh: space: 16 (over z_hi, x, core), band: 8 (over z_lo, y).
Axes of the slice: x: 4, y: 4, z: 4 (z_hi: 2, z_lo: 2; z = z_hi * 2 + z_lo), core: 2. Of those that a mesh axis runs over, the one named last changes fastest.
Arguments:
- blocks: float32 [2, 32, 64, 6144], P(None, 'band', 'space'), may hold values from -304 to 304
- later: float32 [256, 64, 6144], P('band', 'space'), may hold values from -304 to 304
- potential: float32 [64, 6144], P('space'), may hold values from -1.5 to 1.5
Outputs:
- h_block: float32 [2, 32, 64, 6144], P(None, 'band', 'space')
- h_later: float32 [256, 64, 6144], P('band', 'space')
All inputs are finite; a program needn't handle non-finite values.
Results may differ from a plain program's by a relative error of at most 0.00009.
Values sent between devices are 32-bit elements; how exact they have to be, the bound alone decides.
A program may use at most 128 MiB of HBM per device.

v0:
```python
import jax
import jax.numpy as jnp
from jax import lax
from jax.sharding import PartitionSpec as P

NZ = 96


stencil_weights = (-205.0 / 72.0, 8.0 / 5.0, -1.0 / 5.0, 8.0 / 315.0, -1.0 / 560.0)


def extended_2(x, sides, width):
    for axis, dim in sides:
        size, length = (lax.axis_size(axis), x.shape[dim])
        up = [(i, (i + 1) % size) for i in range(size - 1)]
        down = [(j, i) for i, j in up]
        last = lax.slice_in_dim(x, length - width, length, axis=dim)
        initial = lax.slice_in_dim(x, 0, width, axis=dim)
        before = lax.ppermute(last, axis, up)
        after = lax.ppermute(initial, axis, down)
        x = jnp.concatenate([before, x, after], axis=dim)
    return x


def stencil(extended, potential, depth):
    center = extended[:, 4:-4]
    planes = center.shape[1]
    length = center.shape[2]
    laplace = 3.0 * stencil_weights[0] * center
    for step in range(1, 5):
        laplace = laplace + stencil_weights[step] * (
            extended[:, 4 + step : 4 + step + planes] + extended[:, 4 - step : 4 - step + planes]
        )
    margin = 4 * depth
    ypadded = jnp.pad(center, ((0, 0), (0, 0), (margin, margin)))
    for step in range(1, 5):
        upper = ypadded[:, :, margin + step * depth : margin + step * depth + length]
        lower = ypadded[:, :, margin - step * depth : margin - step * depth + length]
        laplace = laplace + stencil_weights[step] * (upper + lower)
    zpadded = jnp.pad(center, ((0, 0), (0, 0), (4, 4)))
    zpos = lax.broadcasted_iota(jnp.int32, (length,), 0) % depth
    for step in range(1, 5):
        upper = jnp.where(zpos + step < depth, zpadded[:, :, 4 + step : 4 + step + length], 0.0)
        lower = jnp.where(zpos - step >= 0, zpadded[:, :, 4 - step : 4 - step + length], 0.0)
        laplace = laplace + stencil_weights[step] * (upper + lower)
    return -0.5 * laplace + potential[None] * center


def inner(left, right):
    return jnp.dot(
        left, right.T, precision=lax.Precision.HIGHEST, preferred_element_type=jnp.float32
    )


def apply_rows(left, right):
    return jnp.dot(left, right, precision=lax.Precision.HIGHEST, preferred_element_type=jnp.float32)


def local(blocks, later, potential):
    own_rows = blocks.shape[1]
    planes = blocks.shape[2]
    length = blocks.shape[3]
    local_cells = planes * length
    cells = planes * lax.axis_size("space") * length
    later_count = later.shape[0]
    owned = 2 * own_rows
    offset = lax.axis_index("band") * own_rows
    later_flat = later.reshape(later_count, local_cells)
    gathered = lax.all_gather(blocks, "band", axis=1, tiled=True)
    block_rows = gathered.shape[1]
    flat = gathered.reshape(2, block_rows, local_cells)

    def orthonormal(rows):
        correlation = lax.psum(inner(rows, rows), "space") / cells
        lower = jnp.linalg.cholesky(correlation)
        return (lower, lax.linalg.triangular_solve(lower, rows, left_side=True, lower=True))

    lower_one, q_first = orthonormal(flat[0])
    crossed = lax.psum(inner(q_first, flat[1]), "space") / cells
    remainder = flat[1] - apply_rows(crossed.T, q_first)
    lower_two, q_second = orthonormal(remainder)
    weight_one = lax.psum(inner(q_first, later_flat), "space") / cells
    partial_later = later_flat - apply_rows(weight_one.T, q_first)
    weight_two = lax.psum(inner(q_second, partial_later), "space") / cells
    projected = partial_later - apply_rows(weight_two.T, q_second)
    mine_one = lax.dynamic_slice_in_dim(q_first, offset, own_rows, 0)
    mine_two = lax.dynamic_slice_in_dim(q_second, offset, own_rows, 0)
    states = jnp.concatenate([mine_one, mine_two, projected], axis=0).reshape(
        owned + later_count, planes, length
    )
    extended = extended_2(states, (("space", 1),), 4)
    applied = stencil(extended, potential, NZ)
    h_block = applied[:owned].reshape(blocks.shape)
    h_later = applied[owned:]
    return (h_block, h_later)


def solution(mesh):
    return jax.shard_map(
        local,
        mesh=mesh,
        in_specs=(P(None, "band", "space", None), P("band", "space", None), P("space", None)),
        out_specs=(P(None, "band", "space", None), P("band", "space", None)),
        check_vma=False,
    )
```

profile of v0, /device:TPU:64, one launch (start us, length us, event | category | flops | bytes accessed | tf_op | source)
XLA Modules:
  0.0 556.0 jit_solution(2565554386587875953)
XLA Ops:
  9.3 5.4 copy.37
  14.7 69.3 %all-gather.2.cloned.1.call-done = f32[2,32,4,6144]{3,2,0,1:T(4,128)} async-done(((f32[2,4,4,6144]{3,2,0,1:T(4,128)}), f32[2,32,4,6144]{3,2,0,1:T(4,128)}) %all-gather.2.cloned.1.call-update) | async-done | bytes 6291472 | tf_op jit(solution)/shard_map/all_gather | solution.py:69
  83.9 3.3 fusion.56
  87.2 3.5 copy.36
  90.7 4.2 fusion.35
  94.9 67.4 %psum.35 = f32[32,32]{0,1:T(8,128)S(1)} all-reduce(f32[32,32]{0,1:T(8,128)S(1)} %fusion.35), channel_id=1, replica_groups=mesh['space'=16,'band'=8] {'space'}, use_global_device_ids=true, to_apply=%region_0.0 | all-reduce | flops 1024 | bytes 8192 | tf_op jit(solution)/shard_map/psum | solution.py:74
  162.4 2.9 cholesky.44
  170.9 2.8 fusion.44
  173.7 2.7 fusion.57
  176.5 65.2 %psum.36 = f32[32,32]{0,1:T(8,128)S(1)} all-reduce(f32[32,32]{0,1:T(8,128)S(1)} %fusion.57), channel_id=1, replica_groups=mesh['space'=16,'band'=8] {'space'}, use_global_device_ids=true, to_apply=%region_3.6 | all-reduce | flops 1024 | bytes 8192 | tf_op jit(solution)/shard_map/psum | solution.py:79
  241.7 4.9 convolution_subtract_fusion.2
  250.9 3.3 fusion.59
  254.2 66.6 %all-reduce.2 = (f32[32,32]{0,1:T(8,128)}, f32[32,32]{0,1:T(8,128)}) all-reduce(f32[32,32]{0,1:T(8,128)} %fusion.59, f32[32,32]{0,1:T(8,128)S(1)} %fusion.58), channel_id=1, replica_groups=mesh['space'=16,'band'=8] {'space'}, use_global_device_ids=true, to_apply=%region_5.8 | all-reduce | flops 2048 | bytes 16384 | tf_op jit(solution)/shard_map/psum | solution.py:82
  320.8 5.4 convolution_subtract_fusion.1
  326.3 2.9 cholesky.55
  333.0 4.8 fusion.41
  338.7 3.3 fusion.60
  342.0 65.7 %psum.39 = f32[32,32]{0,1:T(8,128)S(1)} all-reduce(f32[32,32]{0,1:T(8,128)} %fusion.60), channel_id=1, replica_groups=mesh['space'=16,'band'=8] {'space'}, use_global_device_ids=true, to_apply=%region_6.9 | all-reduce | flops 1024 | bytes 8192 | tf_op jit(solution)/shard_map/psum | solution.py:84
  407.7 4.7 convolution_subtract_fusion
  414.6 5.7 %reshape.36 = f32[40,4,6144]{2,1,0:T(4,128)} reshape(f32[40,24576]{1,0:T(8,128)} %pad_maximum_fusion.2) | data formatting | bytes 7864320 | tf_op jit(solution)/shard_map/reshape | solution.py:88
  424.9 40.8 %collective-permute-done = f32[40,4,6144]{2,1,0:T(4,128)} collective-permute-done((f32[40,4,6144]{2,1,0:T(4,128)}, f32[40,4,6144]{2,1,0:T(4,128)}, u32[]{:S(2)}, u32[]{:S(2)}) %collective-permute-start) | collective-permute-done | bytes 3932192 | tf_op jit(solution)/shard_map/ppermute | solution.py:20
  465.7 7.4 %collective-permute-done.1 = f32[40,4,6144]{2,1,0:T(4,128)} collective-permute-done((f32[40,4,6144]{2,1,0:T(4,128)}, f32[40,4,6144]{2,1,0:T(4,128)}, u32[]{:S(2)}, u32[]{:S(2)}) %collective-permute-start.1) | collective-permute-done | bytes 3932192 | tf_op jit(solution)/shard_map/ppermute | solution.py:19
  473.1 69.8 %multiply_add_fusion = f32[40,4,6144]{2,1,0:T(4,128)} fusion(f32[40,4,6144]{2,1,0:T(4,128)} %reshape.36, f32[40,4,6144]{2,1,0:T(4,128)} %collective-permute-done.1, f32[40,4,6144]{2,1,0:T(4,128)} %collective-permute-done, f32[4,6144]{1,0:T(4,128)S(1)} %copy-done.5, pred[6144]{0:T(1024)(128)(4,1)S(1)} %get-tuple-element.8, ...), kind=kLoop, calls=%fused_computation.33 | loop fusion | flops 53084160 | bytes 15876096 | tf_op jit(solution)/shard_map/add | solution.py:46
  545.0 3.9 slice.130
  (43 shorter events, 25.7 us)
Async XLA Ops:
  7.2 76.8 %all-gather.2.cloned.1.call-start = ((), (), s32[]{:S(2)}) async-start(), calls=%async_computation | async-start | bytes 7077888 | tf_op jit(solution)/shard_map/all_gather | solution.py:69
  170.9 2.8 copy-start.2
  246.5 1.7 copy-start
  248.2 2.7 copy-start.1
  320.8 5.4 copy-start.6
  333.0 5.7 %copy-start.3 = (f32[32,24576]{1,0:T(8,128)S(1)}, f32[32,24576]{1,0:T(8,128)}, u32[]{:S(2)}) copy-start(f32[32,24576]{1,0:T(8,128)} %convolution_subtract_fusion.1) | copy-start | bytes 9437188
  407.7 4.7 copy-start.4
  414.6 58.5 %copy-start.5 = (f32[4,6144]{1,0:T(4,128)S(1)}, f32[4,6144]{1,0:T(4,128)}, u32[]{:S(2)}) copy-start(f32[4,6144]{1,0:T(4,128)} %param.8) | copy-start | bytes 294916
  420.3 45.4 %collective-permute-start = (f32[40,4,6144]{2,1,0:T(4,128)}, f32[40,4,6144]{2,1,0:T(4,128)}, u32[]{:S(2)}, u32[]{:S(2)}) collective-permute-start(f32[40,4,6144]{2,1,0:T(4,128)} %reshape.36), channel_id=1, source_target_pairs={{8,0},{16,8},{24,16},{32,24},{40,32},{48,40},{56,48},{64,56},{72,6... | collective-permute-start | bytes 11796488 | tf_op jit(solution)/shard_map/ppermute | solution.py:20
  422.2 50.9 %collective-permute-start.1 = (f32[40,4,6144]{2,1,0:T(4,128)}, f32[40,4,6144]{2,1,0:T(4,128)}, u32[]{:S(2)}, u32[]{:S(2)}) collective-permute-start(f32[40,4,6144]{2,1,0:T(4,128)} %reshape.36), channel_id=1, source_target_pairs={{0,8},{8,16},{16,24},{24,32},{32,40},{40,48},{48,56},{56,64},{64,7... | collective-permute-start | bytes 11796488 | tf_op jit(solution)/shard_map/ppermute | solution.py:19
Sparse Core Ops, SparseCore 0:
  10.2 73.6 all-gather.1
where the time goes:
time: 563 us; the launch traced here: 556 us
  blocking collectives  265 us (47%)
  waiting for transfers between devices  117 us (21%)
  other arithmetic  85.5 us (15%)
  matrix products  38.7 us (7%)
  local copies, waits for them, and re-layouts  30.4 us (5%)
  between operations  14.5 us (3%)
    add x1, other arithmetic, stencil(): return -0.5 * laplace + potential[None] * center  69.8 us
    all_gather x1, waiting for transfers between devices, local(): gathered = lax.all_gather(blocks, 'band', axis=1, tiled=True)  69.3 us
    psum x1, blocking collectives, orthonormal(): correlation = lax.psum(inner(rows, rows), 'space') / cells  67.4 us
    psum x1, blocking collectives, local(): weight_one = lax.psum(inner(q_first, later_flat), 'space') / cells  66.6 us
    psum x1, blocking collectives, local(): weight_two = lax.psum(inner(q_second, partial_later), 'space') / cells  65.7 us
    psum x1, blocking collectives, local(): crossed = lax.psum(inner(q_first, flat[1]), 'space') / cells  65.2 us
    ppermute x1, waiting for transfers between devices, extended_2(): after = lax.ppermute(initial, axis, down)  40.8 us
    dot_general x5, matrix products, inner(): jnp.dot(left, right.T, precision=lax.Precision.HIGHEST, preferred_element...  16.1 us
  transfers between devices with their start and end apart: 3, of which 3 were waited for; matrix products, arithmetic and copies ran while one was open for 1% of the time, Pallas kernels for 0%

commit v1 on v0

v1 whole, which is shorter than its diff:
```python
import functools

import jax
import jax.numpy as jnp
from jax import lax
from jax.experimental import pallas as pl
from jax.experimental.pallas import tpu as pltpu
from jax.sharding import PartitionSpec as P

MESH = pl.DeviceIdType.MESH
F32 = jnp.float32
BF16 = jnp.bfloat16
NZ = 96
ROWS = 192
PAD = 16
PITCH = ROWS + 2 * PAD
CHUNKS = 4
CROWS = ROWS // CHUNKS
NB = 8
NL = 32
ALL = 64
weights = (-205.0 / 72.0, 8.0 / 5.0, -1.0 / 5.0, 8.0 / 315.0, -1.0 / 560.0)


def lanes(shape=(8, 128)):
    return lax.broadcasted_iota(jnp.int32, shape, len(shape) - 1)


def split(value):
    high = value.astype(BF16)
    return high, (value - high.astype(F32)).astype(BF16)


def stencil(own, left, right, pot, group, out):
    ref, base = out
    lane = lanes()

    def load(chunk, plane):
        return own[pl.ds(group * (8 * PITCH) + PAD + 4 * chunk + plane, 8, stride=PITCH), :]

    def shifted(row, shift):
        q, e = shift // 128, shift % 128
        if e == 0:
            return row[q + 3]
        mixed = jnp.where(lane >= e, row[q + 3], row[q + 4])
        return pltpu.roll(mixed, 128 - e, 1)

    def one(chunk, third):
        zpos = lane + 32 * third
        zpos = jnp.where(zpos >= NZ, zpos - NZ, zpos)
        rows = [[load(chunk + d, plane) for d in range(-3, 4)] for plane in range(4)]
        halo = group * (8 * ROWS) + 4 * chunk
        xs = [left[pl.ds(halo + plane, 8, stride=ROWS), :] for plane in range(4)]
        xs += [rows[plane][3] for plane in range(4)]
        xs += [right[pl.ds(halo + plane, 8, stride=ROWS), :] for plane in range(4)]
        for plane in range(4):
            row = rows[plane]
            acc = (pot[pl.ds(4 * chunk + plane, 1), :] - 1.5 * weights[0]) * row[3]
            for k in range(1, 5):
                part = xs[4 + plane + k] + xs[4 + plane - k]
                part = part + (shifted(row, NZ * k) + shifted(row, -NZ * k))
                up = jnp.where(zpos < NZ - k, shifted(row, k), 0.0)
                down = jnp.where(zpos >= k, shifted(row, -k), 0.0)
                acc = acc + (-0.5 * weights[k]) * (part + (up + down))
            ref[pl.ds(base + 4 * chunk + plane, 8, stride=ROWS), :] = acc

    def body(step, carry):
        for third in range(3):
            one(3 * step + third, third)
        return carry

    lax.fori_loop(0, ROWS // 12, body, 0)


def kernel(blk, lat, pot, hb_out, hl_out,
           gath, own3, left3, right3, hown, hacc3, oblk,
           acc, gs, rbuf, red, full, m1, m2, lhs,
           loc_sem, ag_send, ag_recv, halo_send, halo_recv, rs_send, rs_recv, bc_send, bc_recv, out_sem):
    space = lax.axis_index("space")
    band = lax.axis_index("band")
    z, y = band // 4, band % 4

    def at(dy, dz):
        return lax.rem(z + dz, 2) * 4 + lax.rem(y + dy + 4, 4)

    own = own3.reshape(40 * PITCH, 128)
    left = left3.reshape(40 * ROWS, 128)
    right = right3.reshape(40 * ROWS, 128)
    hacc = hacc3.reshape(NL * ROWS, 128)
    hown2 = hown.reshape(NB * ROWS, 128)
    oblk2 = oblk.reshape(NB * ROWS, 128)
    bmat = gath.at[0].reshape(ALL * ROWS, 128)
    hmat = gath.at[1].reshape(ALL * ROWS, 128)

    barrier = pltpu.get_barrier_semaphore()
    for b in (at(1, 0), at(-1, 0), at(0, 1)):
        pl.semaphore_signal(barrier, inc=1, device_id={"band": b}, device_id_type=MESH)

    @pl.loop(1, 16)
    def _(k):
        pl.semaphore_signal(barrier, inc=1, device_id={"space": lax.rem(space + k, 16)}, device_id_type=MESH)

    local_copies = [
        pltpu.make_async_copy(blk.at[0], own3.at[pl.ds(0, 4), pl.ds(PAD, ROWS), :], loc_sem.at[0]),
        pltpu.make_async_copy(blk.at[1], own3.at[pl.ds(4, 4), pl.ds(PAD, ROWS), :], loc_sem.at[1]),
        pltpu.make_async_copy(lat, own3.at[pl.ds(8, NL), pl.ds(PAD, ROWS), :], loc_sem.at[2]),
        pltpu.make_async_copy(blk, gath.at[0, :, pl.ds(4 * band, 4), :, :], loc_sem.at[3]),
    ]
    for copy in local_copies:
        copy.start()
    pl.semaphore_wait(barrier, 18)

    def halo(part, side):
        src = blk.at[part] if part < 2 else lat.at[pl.ds(8 * (part - 2), 8)]
        first, count = (4 * part, 4) if part < 2 else (8 * (part - 1), 8)
        ref = left3 if side == 0 else right3
        return pltpu.make_async_remote_copy(
            src_ref=src, dst_ref=ref.at[pl.ds(first, count)],
            send_sem=halo_send.at[part, side], recv_sem=halo_recv.at[part, side],
            device_id={"space": space + 1 if side == 0 else space - 1}, device_id_type=MESH)

    def halo_start(parts):
        @pl.when(space < 15)
        def _():
            for part in parts:
                halo(part, 0).start()

        @pl.when(space > 0)
        def _():
            for part in parts:
                halo(part, 1).start()

    def halo_wait(parts):
        @pl.when(space > 0)
        def _():
            for part in parts:
                halo(part, 0).wait_recv()

        @pl.when(space < 15)
        def _():
            for part in parts:
                halo(part, 1).wait_recv()

    def halo_sent(parts):
        @pl.when(space < 15)
        def _():
            for part in parts:
                halo(part, 0).wait_send()

        @pl.when(space > 0)
        def _():
            for part in parts:
                halo(part, 1).wait_send()

    def slot(u, b):
        return gath.at[u // CHUNKS, :, pl.ds(4 * b, 4), pl.ds(CROWS * (u % CHUNKS), CROWS), :]

    def move(u, sid):
        even = u % 2 == 0
        source, to = {
            0: ((0, 0), (1, 0)), 1: ((0, 0), (-1, 0)), 2: ((0, 0), (0, 1)),
            3: ((-1, 0), (1, 0)) if even else ((1, 0), (-1, 0)),
            4: ((0, 1), (1, 0)), 5: ((0, 1), (-1, 0)), 6: ((2, 0), (0, 1)),
        }[sid]
        place = slot(u, at(*source))
        if sid < 3:
            part = blk if u < CHUNKS else hown
            src = part.at[:, :, pl.ds(CROWS * (u % CHUNKS), CROWS), :]
        else:
            src = place
        return pltpu.make_async_remote_copy(
            src_ref=src, dst_ref=place, send_sem=ag_send.at[u, sid], recv_sem=ag_recv.at[u, sid],
            device_id={"band": at(*to)}, device_id_type=MESH)

    def start_own(u):
        for sid in (0, 1, 2):
            move(u, sid).start()

    def forward(u):
        move(u, 2).wait_recv()
        move(u, 4).start()
        move(u, 5).start()
        move(u, 0 if u % 2 == 0 else 1).wait_recv()
        move(u, 3).start()

    def across(u):
        move(u, 3).wait_recv()
        move(u, 6).start()

    def arrived(u):
        for sid in (1 if u % 2 == 0 else 0, 4, 5, 6):
            move(u, sid).wait_recv()

    def gram(c):
        def body(step, carry):
            j4 = 4 * (12 * c + step)
            rows = jnp.concatenate([
                jnp.concatenate([bmat[pl.ds(j4 + p, ALL, stride=ROWS), :],
                                 own[pl.ds(8 * PITCH + PAD + j4 + p, NL, stride=PITCH), :]], axis=0)
                for p in range(4)], axis=1)
            high, low = split(rows)
            zero = jnp.zeros((32, 512), BF16)
            a = jnp.concatenate([high[:ALL], low[:ALL]], axis=0)
            b = jnp.concatenate([high, zero, low, zero], axis=0)
            acc[...] += lax.dot_general(a, b, (((1,), (1,)), ((), ())), preferred_element_type=F32)
            return carry

        lax.fori_loop(0, 12, body, 0)

    halo_start((0, 1))
    start_own(0)
    start_own(1)
    for copy in local_copies:
        copy.wait()

    @pl.loop(0, 40)
    def _(o):
        own3[o, pl.ds(0, PAD), :] = jnp.zeros((PAD, 128), F32)
        own3[o, pl.ds(PAD + ROWS, PAD), :] = jnp.zeros((PAD, 128), F32)

    @pl.when(space == 0)
    def _():
        left3[...] = jnp.zeros(left3.shape, F32)

    @pl.when(space == 15)
    def _():
        right3[...] = jnp.zeros(right3.shape, F32)

    acc[...] = jnp.zeros(acc.shape, F32)

    forward(0)
    start_own(2)
    halo_wait((0, 1))
    halo_start((2, 3, 4, 5))
    stencil(own, left, right, pot, 0, (hown2, 0))
    keep = pltpu.make_async_copy(hown, gath.at[1, :, pl.ds(4 * band, 4), :, :], loc_sem.at[4])
    keep.start()
    forward(1)
    across(0)
    start_own(3)
    forward(2)
    across(1)
    start_own(4)
    arrived(0)
    gram(0)
    forward(3)
    across(2)
    start_own(5)
    arrived(1)
    gram(1)
    forward(4)
    across(3)
    start_own(6)
    arrived(2)
    gram(2)
    arrived(3)
    gram(3)

    gs[...] = acc[:, :128] + acc[:, 128:]

    def scatter(k):
        peer = lax.rem(space + k, 16)
        return pltpu.make_async_remote_copy(
            src_ref=gs.at[pl.ds(8 * peer, 8), :], dst_ref=rbuf.at[space],
            send_sem=rs_send.at[k], recv_sem=rs_recv.at[k], device_id={"space": peer}, device_id_type=MESH)

    def spread(k):
        peer = lax.rem(space + k, 16)
        return pltpu.make_async_remote_copy(
            src_ref=red, dst_ref=full.at[pl.ds(8 * space, 8), :],
            send_sem=bc_send.at[k], recv_sem=bc_recv.at[k], device_id={"space": peer}, device_id_type=MESH)

    for k in range(1, 16):
        scatter(k).start()
    rbuf[pl.ds(space, 1)] = gs[pl.ds(8 * space, 8), :][None]
    forward(5)
    across(4)
    start_own(7)
    for k in range(1, 16):
        scatter(k).wait_recv()
    red[...] = jnp.sum(rbuf[...], axis=0)
    for k in range(1, 16):
        spread(k).start()
    full[pl.ds(8 * space, 8), :] = red[...]
    halo_wait((2,))
    stencil(own, left, right, pot, 1, (hacc, 0))
    for k in range(1, 16):
        spread(k).wait_recv()

    cells = 16.0 * ROWS * 128
    m1[...] = (full[pl.ds(0, ALL), :] + full[pl.ds(ALL, ALL), :]) * (1.0 / cells)
    lane64 = lanes((ALL, 128))
    row64 = lax.broadcasted_iota(jnp.int32, (ALL, 128), 0)
    m2[...] = jnp.where((lane64 == row64) | (lane64 == row64 + ALL), 1.0, 0.0).astype(F32)
    lane1 = lanes((1, 128))

    def eliminate(k, carry):
        one, two = m1[pl.ds(k, 1), :], m2[pl.ds(k, 1), :]
        pivot = jnp.sum(jnp.where(lane1 == k, one, 0.0), axis=1, keepdims=True)
        whole = m1[...]
        column = jnp.sum(jnp.where(lane64 == k, whole, 0.0), axis=1, keepdims=True)
        factor = jnp.where(row64[:, :1] > k, column / pivot, 0.0)
        m1[...] = whole - factor * one
        m2[...] = m2[...] - factor * two
        return carry

    lax.fori_loop(0, 32, eliminate, 0)
    forward(6)
    across(5)
    lax.fori_loop(32, 64, eliminate, 0)
    forward(7)
    across(6)
    diag = jnp.sum(jnp.where(lane64 == row64, m1[...], 0.0), axis=1, keepdims=True)
    scale = 1.0 / jnp.sqrt(diag)
    tri = m2[...] * scale
    proj = lax.dot_general(m1[...] * scale, tri, (((0,), (0,)), ((), ())),
                           precision=lax.Precision.HIGHEST, preferred_element_type=F32)
    row8 = lax.broadcasted_iota(jnp.int32, (8, ALL), 0)
    wanted = jnp.where(row8 < 4, row8, row8 + 28) + 4 * band
    pick = jnp.where(lanes((8, ALL)) == wanted, 1.0, 0.0).astype(F32)
    mine = jnp.dot(pick, tri, precision=lax.Precision.HIGHEST, preferred_element_type=F32)
    coef = jnp.concatenate([mine, -proj[64:96], jnp.zeros((8, 128), F32)], axis=0)
    high = coef.astype(BF16).astype(F32)
    mixed = jnp.where(lanes((48, 128)) < 64, high, coef - high).astype(BF16)
    lhs[...] = jnp.concatenate([mixed, mixed], axis=1)
    halo_wait((3, 4, 5))
    lax.fori_loop(1, 4, lambda g, carry: (
        stencil(own, left, right, pot, g + 1, (hacc, g * (8 * ROWS))), carry)[1], 0)
    across(7)
    keep.wait()

    outs = []
    for c in range(CHUNKS):
        arrived(CHUNKS + c)

        def body(step, carry, c=c):
            j4 = 4 * (12 * c + step)
            rows = jnp.concatenate([hmat[pl.ds(j4 + p, ALL, stride=ROWS), :] for p in range(4)], axis=1)
            high, low = split(rows)
            rhs = jnp.concatenate([high, high, low, low], axis=0)
            res = jnp.dot(lhs[...], rhs, preferred_element_type=F32)
            for p in range(4):
                piece = res[:, 128 * p:128 * p + 128]
                oblk2[pl.ds(j4 + p, 8, stride=ROWS), :] = piece[:8]
                for g in range(4):
                    where = pl.ds(g * (8 * ROWS) + j4 + p, 8, stride=ROWS)
                    hacc[where, :] = hacc[where, :] + piece[8 + 8 * g:16 + 8 * g]
            return carry

        lax.fori_loop(0, 12, body, 0)
        span = pl.ds(CROWS * c, CROWS)
        outs.append(pltpu.make_async_copy(oblk.at[:, :, span, :], hb_out.at[:, :, span, :], out_sem.at[0, c]))
        outs.append(pltpu.make_async_copy(hacc3.at[:, span, :], hl_out.at[:, span, :], out_sem.at[1, c]))
        outs[-2].start()
        outs[-1].start()

    halo_sent((0, 1, 2, 3, 4, 5))
    for u in range(2 * CHUNKS):
        for sid in range(7):
            move(u, sid).wait_send()
    for k in range(1, 16):
        scatter(k).wait_send()
        spread(k).wait_send()
    for copy in outs:
        copy.wait()


def rows_of(x):
    lead = x.shape[:-2]
    x = x.reshape(*lead, 4, 48, 128)
    return jnp.swapaxes(x, -3, -2).reshape(*lead, ROWS, 128)


def planes_of(x):
    lead = x.shape[:-2]
    x = jnp.swapaxes(x.reshape(*lead, 48, 4, 128), -3, -2)
    return x.reshape(*lead, 4, 48 * 128)


def local(blocks, later, potential):
    hb, hl = pl.pallas_call(
        kernel,
        out_shape=[jax.ShapeDtypeStruct((2, 4, ROWS, 128), F32), jax.ShapeDtypeStruct((NL, ROWS, 128), F32)],
        in_specs=[pl.BlockSpec(memory_space=pl.ANY), pl.BlockSpec(memory_space=pl.ANY),
                  pl.BlockSpec(memory_space=pltpu.VMEM)],
        out_specs=[pl.BlockSpec(memory_space=pl.ANY), pl.BlockSpec(memory_space=pl.ANY)],
        scratch_shapes=[
            pltpu.VMEM((2, 2, 32, ROWS, 128), F32),
            pltpu.VMEM((40, PITCH, 128), F32),
            pltpu.VMEM((40, ROWS, 128), F32),
            pltpu.VMEM((40, ROWS, 128), F32),
            pltpu.VMEM((2, 4, ROWS, 128), F32),
            pltpu.VMEM((NL, ROWS, 128), F32),
            pltpu.VMEM((2, 4, ROWS, 128), F32),
            pltpu.VMEM((128, 256), F32),
            pltpu.VMEM((128, 128), F32),
            pltpu.VMEM((16, 8, 128), F32),
            pltpu.VMEM((8, 128), F32),
            pltpu.VMEM((128, 128), F32),
            pltpu.VMEM((ALL, 128), F32),
            pltpu.VMEM((ALL, 128), F32),
            pltpu.VMEM((48, 256), BF16),
            pltpu.SemaphoreType.DMA((5,)),
            pltpu.SemaphoreType.DMA((8, 7)),
            pltpu.SemaphoreType.DMA((8, 7)),
            pltpu.SemaphoreType.DMA((6, 2)),
            pltpu.SemaphoreType.DMA((6, 2)),
            pltpu.SemaphoreType.DMA((16,)),
            pltpu.SemaphoreType.DMA((16,)),
            pltpu.SemaphoreType.DMA((16,)),
            pltpu.SemaphoreType.DMA((16,)),
            pltpu.SemaphoreType.DMA((2, 4)),
        ],
        compiler_params=pltpu.CompilerParams(
            collective_id=0, has_side_effects=True, vmem_limit_bytes=56 * 1024 * 1024),
    )(rows_of(blocks), rows_of(later), rows_of(potential))
    return planes_of(hb), planes_of(hl)


def solution(mesh):
    return jax.shard_map(
        local,
        mesh=mesh,
        in_specs=(P(None, "band", "space", None), P("band", "space", None), P("space", None)),
        out_specs=(P(None, "band", "space", None), P("band", "space", None)),
        check_vma=False,
    )
```

time: 563 us -> 167 us (0.30)
  the two profiles are of different devices: /device:TPU:64 before, /device:TPU:0 now
where the time goes in v1:
time: 167 us
  Pallas kernels  160 us (96%)
  local copies, waits for them, and re-layouts  5.96 us (4%)
    pallas_call x1, Pallas kernels, local(): pl.pallas_call(kernel, out_shape=[jax.ShapeDtypeStruct((2, 4, ROWS, 128),...  160 us
    unnamed x2, local copies, waits for them, and re-layouts  5.96 us

profile of v1, /device:TPU:0, one launch (start us, length us, event | category | flops | bytes accessed | tf_op | source)
XLA Modules:
  0.0 166.9 jit_solution(1752372045390510897)
XLA Ops:
  0.6 160.3 %shard_map.50 = (f32[2,4,192,128]{3,2,1,0:T(8,128)}, f32[32,192,128]{2,1,0:T(8,128)}) custom-call(f32[2,4,192,128]{3,2,1,0:T(8,128)} %bitcast.28, f32[32,192,128]{2,1,0:T(8,128)} %bitcast.26, f32[192,128]{1,0:T(8,128)} %bitcast.29), custom_call_target="tpu_custom_call" | custom-call | tf_op jit(solution)/shard_map/pallas_call | solution.py:381
  161.0 2.1 %copy.12 = f32[2,4,4,6144]{3,2,1,0:T(4,128)} copy(f32[2,4,4,6144]{3,2,1,0:T(4,128)} %bitcast.27) | data formatting | bytes 1572864
  163.1 3.9 %copy.13 = f32[32,4,6144]{2,1,0:T(4,128)} copy(f32[32,4,6144]{2,1,0:T(4,128)} %bitcast.25) | data formatting | bytes 6291456

commit v2 on v1

--- a/solution.py
+++ b/solution.py
@@ -18,6 +18,7 @@
 CROWS = ROWS // CHUNKS
 NB = 8
 NL = 32
+VIA = 5
 ALL = 64
 weights = (-205.0 / 72.0, 8.0 / 5.0, -1.0 / 5.0, 8.0 / 315.0, -1.0 / 560.0)
 
@@ -73,9 +74,9 @@
 
 
 def kernel(blk, lat, pot, hb_out, hl_out,
-           gath, own3, left3, right3, hown, hacc3, oblk,
+           gath, own3, left3, right3, relay, hown, hacc3, oblk,
            acc, gs, rbuf, red, full, m1, m2, lhs,
-           loc_sem, ag_send, ag_recv, halo_send, halo_recv, rs_send, rs_recv, bc_send, bc_recv, out_sem):
+           loc_sem, ag_send, ag_recv, halo_send, halo_recv, relay_send, relay_recv, rs_send, rs_recv, bc_send, bc_recv, out_sem):
     space = lax.axis_index("space")
     band = lax.axis_index("band")
     z, y = band // 4, band % 4
@@ -110,47 +111,79 @@
         copy.start()
     pl.semaphore_wait(barrier, 18)
 
+    def source(part):
+        return blk.at[part] if part < 2 else lat.at[pl.ds(4 * (part - 2), 4)]
+
     def halo(part, side):
-        src = blk.at[part] if part < 2 else lat.at[pl.ds(8 * (part - 2), 8)]
-        first, count = (4 * part, 4) if part < 2 else (8 * (part - 1), 8)
         ref = left3 if side == 0 else right3
         return pltpu.make_async_remote_copy(
-            src_ref=src, dst_ref=ref.at[pl.ds(first, count)],
+            src_ref=source(part), dst_ref=ref.at[pl.ds(4 * part, 4)],
             send_sem=halo_send.at[part, side], recv_sem=halo_recv.at[part, side],
             device_id={"space": space + 1 if side == 0 else space - 1}, device_id_type=MESH)
 
+    def detour(part, side):
+        return pltpu.make_async_remote_copy(
+            src_ref=source(part), dst_ref=relay.at[part - VIA],
+            send_sem=halo_send.at[part, side], recv_sem=relay_recv.at[part - VIA],
+            device_id={"space": space + 8 if side == 0 else space - 8}, device_id_type=MESH)
+
+    def onward(part, side):
+        ref = left3 if side == 0 else right3
+        return pltpu.make_async_remote_copy(
+            src_ref=relay.at[part - VIA], dst_ref=ref.at[pl.ds(4 * part, 4)],
+            send_sem=relay_send.at[part - VIA], recv_sem=halo_recv.at[part, side],
+            device_id={"space": space - 7 if side == 0 else space + 7}, device_id_type=MESH)
+
+    senders = ((space < 15, space == 7, space != 7), (space > 0, space == 8, space != 8))
+
+    def halo_each(parts, direct, around):
+        for side, (any_, seam, inner) in enumerate(senders):
+            @pl.when(any_)
+            def _(side=side):
+                for part in parts:
+                    if part < VIA:
+                        direct(part, side)
+
+            if any(part >= VIA for part in parts):
+                @pl.when(any_ & inner)
+                def _(side=side):
+                    for part in parts:
+                        if part >= VIA:
+                            direct(part, side)
+
+                @pl.when(seam)
+                def _(side=side):
+                    for part in parts:
+                        if part >= VIA:
+                            around(part, side)
+
     def halo_start(parts):
-        @pl.when(space < 15)
-        def _():
-            for part in parts:
-                halo(part, 0).start()
-
-        @pl.when(space > 0)
-        def _():
-            for part in parts:
-                halo(part, 1).start()
+        halo_each(parts, lambda p, s: halo(p, s).start(), lambda p, s: detour(p, s).start())
+
+    def halo_sent(parts):
+        halo_each(parts, lambda p, s: halo(p, s).wait_send(), lambda p, s: detour(p, s).wait_send())
 
     def halo_wait(parts):
-        @pl.when(space > 0)
-        def _():
-            for part in parts:
-                halo(part, 0).wait_recv()
-
-        @pl.when(space < 15)
-        def _():
-            for part in parts:
-                halo(part, 1).wait_recv()
-
-    def halo_sent(parts):
-        @pl.when(space < 15)
-        def _():
-            for part in parts:
-                halo(part, 0).wait_send()
-
-        @pl.when(space > 0)
-        def _():
-            for part in parts:
-                halo(part, 1).wait_send()
+        for side, there in enumerate((space > 0, space < 15)):
+            @pl.when(there)
+            def _(side=side):
+                for part in parts:
+                    halo(part, side).wait_recv()
+
+    def pass_on(parts):
+        for side, here in enumerate((space == 15, space == 0)):
+            @pl.when(here)
+            def _(side=side):
+                for part in parts:
+                    detour(part, side).wait_recv()
+                    onward(part, side).start()
+
+    def passed(parts):
+        for side, here in enumerate((space == 15, space == 0)):
+            @pl.when(here)
+            def _(side=side):
+                for part in parts:
+                    onward(part, side).wait_send()
 
     def slot(u, b):
         return gath.at[u // CHUNKS, :, pl.ds(4 * b, 4), pl.ds(CROWS * (u % CHUNKS), CROWS), :]
@@ -207,8 +240,8 @@
 
         lax.fori_loop(0, 12, body, 0)
 
-    halo_start((0, 1))
     start_own(0)
+    halo_start(range(10))
     start_own(1)
     for copy in local_copies:
         copy.wait()
@@ -228,16 +261,19 @@
 
     acc[...] = jnp.zeros(acc.shape, F32)
 
+    def later(g):
+        halo_wait((2 * g, 2 * g + 1))
+        stencil(own, left, right, pot, g, (hacc, (g - 1) * (8 * ROWS)))
+
     forward(0)
     start_own(2)
+    forward(1)
+    across(0)
+    start_own(3)
     halo_wait((0, 1))
-    halo_start((2, 3, 4, 5))
     stencil(own, left, right, pot, 0, (hown2, 0))
     keep = pltpu.make_async_copy(hown, gath.at[1, :, pl.ds(4 * band, 4), :, :], loc_sem.at[4])
     keep.start()
-    forward(1)
-    across(0)
-    start_own(3)
     forward(2)
     across(1)
     start_own(4)
@@ -251,6 +287,7 @@
     forward(4)
     across(3)
     start_own(6)
+    pass_on((5,))
     arrived(2)
     gram(2)
     arrived(3)
@@ -273,17 +310,18 @@
     for k in range(1, 16):
         scatter(k).start()
     rbuf[pl.ds(space, 1)] = gs[pl.ds(8 * space, 8), :][None]
-    forward(5)
-    across(4)
-    start_own(7)
+    later(1)
     for k in range(1, 16):
         scatter(k).wait_recv()
     red[...] = jnp.sum(rbuf[...], axis=0)
     for k in range(1, 16):
         spread(k).start()
     full[pl.ds(8 * space, 8), :] = red[...]
-    halo_wait((2,))
-    stencil(own, left, right, pot, 1, (hacc, 0))
+    forward(5)
+    across(4)
+    start_own(7)
+    pass_on((6, 7))
+    later(2)
     for k in range(1, 16):
         spread(k).wait_recv()
 
@@ -307,9 +345,8 @@
     lax.fori_loop(0, 32, eliminate, 0)
     forward(6)
     across(5)
+    pass_on((8, 9))
     lax.fori_loop(32, 64, eliminate, 0)
-    forward(7)
-    across(6)
     diag = jnp.sum(jnp.where(lane64 == row64, m1[...], 0.0), axis=1, keepdims=True)
     scale = 1.0 / jnp.sqrt(diag)
     tri = m2[...] * scale
@@ -323,9 +360,10 @@
     high = coef.astype(BF16).astype(F32)
     mixed = jnp.where(lanes((48, 128)) < 64, high, coef - high).astype(BF16)
     lhs[...] = jnp.concatenate([mixed, mixed], axis=1)
-    halo_wait((3, 4, 5))
-    lax.fori_loop(1, 4, lambda g, carry: (
-        stencil(own, left, right, pot, g + 1, (hacc, g * (8 * ROWS))), carry)[1], 0)
+    later(3)
+    forward(7)
+    across(6)
+    later(4)
     across(7)
     keep.wait()
 
@@ -354,7 +392,8 @@
         outs[-2].start()
         outs[-1].start()
 
-    halo_sent((0, 1, 2, 3, 4, 5))
+    halo_sent(range(10))
+    passed(range(VIA, 10))
     for u in range(2 * CHUNKS):
         for sid in range(7):
             move(u, sid).wait_send()
@@ -389,6 +428,7 @@
             pltpu.VMEM((40, PITCH, 128), F32),
             pltpu.VMEM((40, ROWS, 128), F32),
             pltpu.VMEM((40, ROWS, 128), F32),
+            pltpu.VMEM((10 - VIA, 4, ROWS, 128), F32),
             pltpu.VMEM((2, 4, ROWS, 128), F32),
             pltpu.VMEM((NL, ROWS, 128), F32),
             pltpu.VMEM((2, 4, ROWS, 128), F32),
@@ -403,8 +443,10 @@
             pltpu.SemaphoreType.DMA((5,)),
             pltpu.SemaphoreType.DMA((8, 7)),
             pltpu.SemaphoreType.DMA((8, 7)),
-            pltpu.SemaphoreType.DMA((6, 2)),
-            pltpu.SemaphoreType.DMA((6, 2)),
+            pltpu.SemaphoreType.DMA((10, 2)),
+            pltpu.SemaphoreType.DMA((10, 2)),
+            pltpu.SemaphoreType.DMA((10 - VIA,)),
+            pltpu.SemaphoreType.DMA((10 - VIA,)),
             pltpu.SemaphoreType.DMA((16,)),
             pltpu.SemaphoreType.DMA((16,)),
             pltpu.SemaphoreType.DMA((16,)),

time: 167 us -> 141 us (0.84)
  Pallas kernels: 160 us -> 133 us
    pallas_call x1, Pallas kernels: 160 us -> 133 us  [local(): pl.pallas_call(kernel, out_shape=[jax.ShapeDtypeStruct((2, 4, ROWS, 128),...]
where the time goes in v2:
time: 141 us; the launch traced here: 140 us
  Pallas kernels  133 us (94%)
  local copies, waits for them, and re-layouts  5.96 us (4%)
    pallas_call x1, Pallas kernels, local(): pl.pallas_call(kernel, out_shape=[jax.ShapeDtypeStruct((2, 4, ROWS, 128),...  133 us
    unnamed x2, local copies, waits for them, and re-layouts  5.96 us

profile of v2, /device:TPU:0, one launch (start us, length us, event | category | flops | bytes accessed | tf_op | source)
XLA Modules:
  0.0 140.1 jit_solution(3974115233828111554)
XLA Ops:
  0.6 133.5 %shard_map.50 = (f32[2,4,192,128]{3,2,1,0:T(8,128)}, f32[32,192,128]{2,1,0:T(8,128)}) custom-call(f32[2,4,192,128]{3,2,1,0:T(8,128)} %bitcast.28, f32[32,192,128]{2,1,0:T(8,128)} %bitcast.26, f32[192,128]{1,0:T(8,128)} %bitcast.29), custom_call_target="tpu_custom_call" | custom-call | tf_op jit(solution)/shard_map/pallas_call | solution.py:420
  134.1 2.1 %copy.12 = f32[2,4,4,6144]{3,2,1,0:T(4,128)} copy(f32[2,4,4,6144]{3,2,1,0:T(4,128)} %bitcast.27) | data formatting | bytes 1572864
  136.2 3.9 %copy.13 = f32[32,4,6144]{2,1,0:T(4,128)} copy(f32[32,4,6144]{2,1,0:T(4,128)} %bitcast.25) | data formatting | bytes 6291456

commit v3 on v2

--- a/solution.py
+++ b/solution.py
@@ -13,9 +13,13 @@
 NZ = 96
 ROWS = 192
 PAD = 16
-PITCH = ROWS + 2 * PAD
-CHUNKS = 4
+PITCH = 216
+STEP = 200
+CHUNKS = 6
 CROWS = ROWS // CHUNKS
+UNITS = 2 * CHUNKS
+HALOS = {0: (0, 1, 5), 1: (6, 2), 2: (7, 3), 3: (8, 4), 4: (9,)}
+PASSES = {6: (5,), 7: (6,), 8: (7,), 9: (8,), 10: (9,)}
 NB = 8
 NL = 32
 VIA = 5
@@ -50,10 +54,10 @@
         zpos = lane + 32 * third
         zpos = jnp.where(zpos >= NZ, zpos - NZ, zpos)
         rows = [[load(chunk + d, plane) for d in range(-3, 4)] for plane in range(4)]
-        halo = group * (8 * ROWS) + 4 * chunk
-        xs = [left[pl.ds(halo + plane, 8, stride=ROWS), :] for plane in range(4)]
+        halo = group * (8 * STEP) + 4 * chunk
+        xs = [left[pl.ds(halo + plane, 8, stride=STEP), :] for plane in range(4)]
         xs += [rows[plane][3] for plane in range(4)]
-        xs += [right[pl.ds(halo + plane, 8, stride=ROWS), :] for plane in range(4)]
+        xs += [right[pl.ds(halo + plane, 8, stride=STEP), :] for plane in range(4)]
         for plane in range(4):
             row = rows[plane]
             acc = (pot[pl.ds(4 * chunk + plane, 1), :] - 1.5 * weights[0]) * row[3]
@@ -63,7 +67,7 @@
                 up = jnp.where(zpos < NZ - k, shifted(row, k), 0.0)
                 down = jnp.where(zpos >= k, shifted(row, -k), 0.0)
                 acc = acc + (-0.5 * weights[k]) * (part + (up + down))
-            ref[pl.ds(base + 4 * chunk + plane, 8, stride=ROWS), :] = acc
+            ref[pl.ds(base + 4 * chunk + plane, 8, stride=STEP), :] = acc
 
     def body(step, carry):
         for third in range(3):
@@ -84,14 +88,14 @@
     def at(dy, dz):
         return lax.rem(z + dz, 2) * 4 + lax.rem(y + dy + 4, 4)
 
-    own = own3.reshape(40 * PITCH, 128)
-    left = left3.reshape(40 * ROWS, 128)
-    right = right3.reshape(40 * ROWS, 128)
-    hacc = hacc3.reshape(NL * ROWS, 128)
-    hown2 = hown.reshape(NB * ROWS, 128)
-    oblk2 = oblk.reshape(NB * ROWS, 128)
-    bmat = gath.at[0].reshape(ALL * ROWS, 128)
-    hmat = gath.at[1].reshape(ALL * ROWS, 128)
+    own = own3.reshape(41 * PITCH, 128)
+    left = left3.reshape(40 * STEP, 128)
+    right = right3.reshape(40 * STEP, 128)
+    hacc = hacc3.reshape(NL * STEP, 128)
+    hown2 = hown.reshape(NB * STEP, 128)
+    oblk2 = oblk.reshape(NB * STEP, 128)
+    bmat = gath.at[0].reshape(ALL * STEP, 128)
+    hmat = gath.at[1].reshape(ALL * STEP, 128)
 
     barrier = pltpu.get_barrier_semaphore()
     for b in (at(1, 0), at(-1, 0), at(0, 1)):
@@ -105,7 +109,7 @@
         pltpu.make_async_copy(blk.at[0], own3.at[pl.ds(0, 4), pl.ds(PAD, ROWS), :], loc_sem.at[0]),
         pltpu.make_async_copy(blk.at[1], own3.at[pl.ds(4, 4), pl.ds(PAD, ROWS), :], loc_sem.at[1]),
         pltpu.make_async_copy(lat, own3.at[pl.ds(8, NL), pl.ds(PAD, ROWS), :], loc_sem.at[2]),
-        pltpu.make_async_copy(blk, gath.at[0, :, pl.ds(4 * band, 4), :, :], loc_sem.at[3]),
+        pltpu.make_async_copy(blk, gath.at[0, :, pl.ds(4 * band, 4), pl.ds(0, ROWS), :], loc_sem.at[3]),
     ]
     for copy in local_copies:
         copy.start()
@@ -117,7 +121,7 @@
     def halo(part, side):
         ref = left3 if side == 0 else right3
         return pltpu.make_async_remote_copy(
-            src_ref=source(part), dst_ref=ref.at[pl.ds(4 * part, 4)],
+            src_ref=source(part), dst_ref=ref.at[pl.ds(4 * part, 4), pl.ds(0, ROWS), :],
             send_sem=halo_send.at[part, side], recv_sem=halo_recv.at[part, side],
             device_id={"space": space + 1 if side == 0 else space - 1}, device_id_type=MESH)
 
@@ -130,7 +134,7 @@
     def onward(part, side):
         ref = left3 if side == 0 else right3
         return pltpu.make_async_remote_copy(
-            src_ref=relay.at[part - VIA], dst_ref=ref.at[pl.ds(4 * part, 4)],
+            src_ref=relay.at[part - VIA], dst_ref=ref.at[pl.ds(4 * part, 4), pl.ds(0, ROWS), :],
             send_sem=relay_send.at[part - VIA], recv_sem=halo_recv.at[part, side],
             device_id={"space": space - 7 if side == 0 else space + 7}, device_id_type=MESH)
 
@@ -226,30 +230,28 @@
 
     def gram(c):
         def body(step, carry):
-            j4 = 4 * (12 * c + step)
+            j4 = CROWS * c + 4 * step
             rows = jnp.concatenate([
-                jnp.concatenate([bmat[pl.ds(j4 + p, ALL, stride=ROWS), :],
+                jnp.concatenate([bmat[pl.ds(j4 + p, ALL, stride=STEP), :],
                                  own[pl.ds(8 * PITCH + PAD + j4 + p, NL, stride=PITCH), :]], axis=0)
                 for p in range(4)], axis=1)
             high, low = split(rows)
-            zero = jnp.zeros((32, 512), BF16)
-            a = jnp.concatenate([high[:ALL], low[:ALL]], axis=0)
-            b = jnp.concatenate([high, zero, low, zero], axis=0)
+            a = jnp.concatenate([high, low], axis=0)
+            b = jnp.concatenate([high[:ALL], low[:ALL]], axis=0)
             acc[...] += lax.dot_general(a, b, (((1,), (1,)), ((), ())), preferred_element_type=F32)
             return carry
 
-        lax.fori_loop(0, 12, body, 0)
+        lax.fori_loop(0, CROWS // 4, body, 0)
 
     start_own(0)
-    halo_start(range(10))
     start_own(1)
     for copy in local_copies:
         copy.wait()
 
-    @pl.loop(0, 40)
+    @pl.loop(0, 41)
     def _(o):
         own3[o, pl.ds(0, PAD), :] = jnp.zeros((PAD, 128), F32)
-        own3[o, pl.ds(PAD + ROWS, PAD), :] = jnp.zeros((PAD, 128), F32)
+        own3[o, pl.ds(PAD + ROWS, 8), :] = jnp.zeros((8, 128), F32)
 
     @pl.when(space == 0)
     def _():
@@ -263,37 +265,38 @@
 
     def later(g):
         halo_wait((2 * g, 2 * g + 1))
-        stencil(own, left, right, pot, g, (hacc, (g - 1) * (8 * ROWS)))
-
-    forward(0)
-    start_own(2)
-    forward(1)
-    across(0)
-    start_own(3)
-    halo_wait((0, 1))
-    stencil(own, left, right, pot, 0, (hown2, 0))
-    keep = pltpu.make_async_copy(hown, gath.at[1, :, pl.ds(4 * band, 4), :, :], loc_sem.at[4])
-    keep.start()
-    forward(2)
-    across(1)
-    start_own(4)
-    arrived(0)
-    gram(0)
-    forward(3)
-    across(2)
-    start_own(5)
-    arrived(1)
-    gram(1)
-    forward(4)
-    across(3)
-    start_own(6)
-    pass_on((5,))
-    arrived(2)
-    gram(2)
-    arrived(3)
-    gram(3)
-
-    gs[...] = acc[:, :128] + acc[:, 128:]
+        stencil(own, left, right, pot, g, (hacc, (g - 1) * (8 * STEP)))
+
+    def step(t):
+        if t < UNITS:
+            forward(t)
+        if 1 <= t:
+            across(t - 1)
+        if t + 2 < UNITS:
+            start_own(t + 2)
+        halo_start(HALOS.get(t, ()))
+        pass_on(PASSES.get(t, ()))
+
+    for t in range(CHUNKS - 2):
+        step(t)
+        if t >= 2:
+            arrived(t - 2)
+            gram(t - 2)
+        if t == CHUNKS - 3:
+            halo_wait((0, 1))
+            stencil(own, left, right, pot, 0, (hown2, 0))
+            keep = pltpu.make_async_copy(hown.at[:, :, pl.ds(0, ROWS), :], gath.at[1, :, pl.ds(4 * band, 4), pl.ds(0, ROWS), :],
+                                         loc_sem.at[4])
+            keep.start()
+    for t in range(CHUNKS - 2, CHUNKS + 2):
+        step(t)
+        if t == CHUNKS:
+            later(1)
+        arrived(t - 2)
+        gram(t - 2)
+
+    gs[pl.ds(0, 96), :] = acc[:96] + acc[96:]
+    gs[pl.ds(96, 32), :] = jnp.zeros((32, 128), F32)
 
     def scatter(k):
         peer = lax.rem(space + k, 16)
@@ -310,23 +313,22 @@
     for k in range(1, 16):
         scatter(k).start()
     rbuf[pl.ds(space, 1)] = gs[pl.ds(8 * space, 8), :][None]
-    later(1)
+    later(2)
+    step(CHUNKS + 2)
     for k in range(1, 16):
         scatter(k).wait_recv()
     red[...] = jnp.sum(rbuf[...], axis=0)
     for k in range(1, 16):
         spread(k).start()
     full[pl.ds(8 * space, 8), :] = red[...]
-    forward(5)
-    across(4)
-    start_own(7)
-    pass_on((6, 7))
-    later(2)
+    later(3)
+    step(CHUNKS + 3)
     for k in range(1, 16):
         spread(k).wait_recv()
 
     cells = 16.0 * ROWS * 128
-    m1[...] = (full[pl.ds(0, ALL), :] + full[pl.ds(ALL, ALL), :]) * (1.0 / cells)
+    total = full[...]
+    m1[...] = jnp.transpose(total + pltpu.roll(total, ALL, 1))[:ALL] * (1.0 / cells)
     lane64 = lanes((ALL, 128))
     row64 = lax.broadcasted_iota(jnp.int32, (ALL, 128), 0)
     m2[...] = jnp.where((lane64 == row64) | (lane64 == row64 + ALL), 1.0, 0.0).astype(F32)
@@ -343,9 +345,7 @@
         return carry
 
     lax.fori_loop(0, 32, eliminate, 0)
-    forward(6)
-    across(5)
-    pass_on((8, 9))
+    step(CHUNKS + 4)
     lax.fori_loop(32, 64, eliminate, 0)
     diag = jnp.sum(jnp.where(lane64 == row64, m1[...], 0.0), axis=1, keepdims=True)
     scale = 1.0 / jnp.sqrt(diag)
@@ -360,11 +360,9 @@
     high = coef.astype(BF16).astype(F32)
     mixed = jnp.where(lanes((48, 128)) < 64, high, coef - high).astype(BF16)
     lhs[...] = jnp.concatenate([mixed, mixed], axis=1)
-    later(3)
-    forward(7)
-    across(6)
+    step(CHUNKS + 5)
     later(4)
-    across(7)
+    step(CHUNKS + 6)
     keep.wait()
 
     outs = []
@@ -372,20 +370,20 @@
         arrived(CHUNKS + c)
 
         def body(step, carry, c=c):
-            j4 = 4 * (12 * c + step)
-            rows = jnp.concatenate([hmat[pl.ds(j4 + p, ALL, stride=ROWS), :] for p in range(4)], axis=1)
+            j4 = CROWS * c + 4 * step
+            rows = jnp.concatenate([hmat[pl.ds(j4 + p, ALL, stride=STEP), :] for p in range(4)], axis=1)
             high, low = split(rows)
             rhs = jnp.concatenate([high, high, low, low], axis=0)
             res = jnp.dot(lhs[...], rhs, preferred_element_type=F32)
             for p in range(4):
                 piece = res[:, 128 * p:128 * p + 128]
-                oblk2[pl.ds(j4 + p, 8, stride=ROWS), :] = piece[:8]
+                oblk2[pl.ds(j4 + p, 8, stride=STEP), :] = piece[:8]
                 for g in range(4):
-                    where = pl.ds(g * (8 * ROWS) + j4 + p, 8, stride=ROWS)
+                    where = pl.ds(g * (8 * STEP) + j4 + p, 8, stride=STEP)
                     hacc[where, :] = hacc[where, :] + piece[8 + 8 * g:16 + 8 * g]
             return carry
 
-        lax.fori_loop(0, 12, body, 0)
+        lax.fori_loop(0, CROWS // 4, body, 0)
         span = pl.ds(CROWS * c, CROWS)
         outs.append(pltpu.make_async_copy(oblk.at[:, :, span, :], hb_out.at[:, :, span, :], out_sem.at[0, c]))
         outs.append(pltpu.make_async_copy(hacc3.at[:, span, :], hl_out.at[:, span, :], out_sem.at[1, c]))
@@ -394,7 +392,7 @@
 
     halo_sent(range(10))
     passed(range(VIA, 10))
-    for u in range(2 * CHUNKS):
+    for u in range(UNITS):
         for sid in range(7):
             move(u, sid).wait_send()
     for k in range(1, 16):
@@ -424,15 +422,15 @@
                   pl.BlockSpec(memory_space=pltpu.VMEM)],
         out_specs=[pl.BlockSpec(memory_space=pl.ANY), pl.BlockSpec(memory_space=pl.ANY)],
         scratch_shapes=[
-            pltpu.VMEM((2, 2, 32, ROWS, 128), F32),
-            pltpu.VMEM((40, PITCH, 128), F32),
-            pltpu.VMEM((40, ROWS, 128), F32),
-            pltpu.VMEM((40, ROWS, 128), F32),
+            pltpu.VMEM((2, 2, 32, STEP, 128), F32),
+            pltpu.VMEM((41, PITCH, 128), F32),
+            pltpu.VMEM((40, STEP, 128), F32),
+            pltpu.VMEM((40, STEP, 128), F32),
             pltpu.VMEM((10 - VIA, 4, ROWS, 128), F32),
-            pltpu.VMEM((2, 4, ROWS, 128), F32),
-            pltpu.VMEM((NL, ROWS, 128), F32),
-            pltpu.VMEM((2, 4, ROWS, 128), F32),
-            pltpu.VMEM((128, 256), F32),
+            pltpu.VMEM((2, 4, STEP, 128), F32),
+            pltpu.VMEM((NL, STEP, 128), F32),
+            pltpu.VMEM((2, 4, STEP, 128), F32),
+            pltpu.VMEM((192, 128), F32),
             pltpu.VMEM((128, 128), F32),
             pltpu.VMEM((16, 8, 128), F32),
             pltpu.VMEM((8, 128), F32),
@@ -441,8 +439,8 @@
             pltpu.VMEM((ALL, 128), F32),
             pltpu.VMEM((48, 256), BF16),
             pltpu.SemaphoreType.DMA((5,)),
-            pltpu.SemaphoreType.DMA((8, 7)),
-            pltpu.SemaphoreType.DMA((8, 7)),
+            pltpu.SemaphoreType.DMA((UNITS, 7)),
+            pltpu.SemaphoreType.DMA((UNITS, 7)),
             pltpu.SemaphoreType.DMA((10, 2)),
             pltpu.SemaphoreType.DMA((10, 2)),
             pltpu.SemaphoreType.DMA((10 - VIA,)),
@@ -451,7 +449,7 @@
             pltpu.SemaphoreType.DMA((16,)),
             pltpu.SemaphoreType.DMA((16,)),
             pltpu.SemaphoreType.DMA((16,)),
-            pltpu.SemaphoreType.DMA((2, 4)),
+            pltpu.SemaphoreType.DMA((2, CHUNKS)),
         ],
         compiler_params=pltpu.CompilerParams(
             collective_id=0, has_side_effects=True, vmem_limit_bytes=56 * 1024 * 1024),

time: 141 us -> 129 us (0.915)
  Pallas kernels: 133 us -> 122 us
    pallas_call x1, Pallas kernels: 133 us -> 122 us  [local(): pl.pallas_call(kernel, out_shape=[jax.ShapeDtypeStruct((2, 4, ROWS, 128),...]
where the time goes in v3:
time: 129 us
  Pallas kernels  122 us (95%)
  local copies, waits for them, and re-layouts  5.96 us (5%)
    pallas_call x1, Pallas kernels, local(): pl.pallas_call(kernel, out_shape=[jax.ShapeDtypeStruct((2, 4, ROWS, 128),...  122 us
    unnamed x2, local copies, waits for them, and re-layouts  5.96 us

profile of v3, /device:TPU:0, one launch (start us, length us, event | category | flops | bytes accessed | tf_op | source)
XLA Modules:
  0.0 128.7 jit_solution(6260712436383571426)
XLA Ops:
  0.6 122.1 %shard_map.50 = (f32[2,4,192,128]{3,2,1,0:T(8,128)}, f32[32,192,128]{2,1,0:T(8,128)}) custom-call(f32[2,4,192,128]{3,2,1,0:T(8,128)} %bitcast.28, f32[32,192,128]{2,1,0:T(8,128)} %bitcast.26, f32[192,128]{1,0:T(8,128)} %bitcast.29), custom_call_target="tpu_custom_call" | custom-call | tf_op jit(solution)/shard_map/pallas_call | solution.py:418
  122.7 2.1 %copy.12 = f32[2,4,4,6144]{3,2,1,0:T(4,128)} copy(f32[2,4,4,6144]{3,2,1,0:T(4,128)} %bitcast.27) | data formatting | bytes 1572864
  124.8 3.9 %copy.13 = f32[32,4,6144]{2,1,0:T(4,128)} copy(f32[32,4,6144]{2,1,0:T(4,128)} %bitcast.25) | data formatting | bytes 6291456

commit v4 on v3

--- a/solution.py
+++ b/solution.py
@@ -18,11 +18,11 @@
 CHUNKS = 6
 CROWS = ROWS // CHUNKS
 UNITS = 2 * CHUNKS
-HALOS = {0: (0, 1, 5), 1: (6, 2), 2: (7, 3), 3: (8, 4), 4: (9,)}
-PASSES = {6: (5,), 7: (6,), 8: (7,), 9: (8,), 10: (9,)}
+HALOS = {0: (0, 3), 1: (1,), 2: (2, 5), 4: (4, 7), 6: (6, 9), 8: (8,)}
+PASSES = {2: (3,), 4: (5,), 6: (7,), 8: (9,)}
 NB = 8
 NL = 32
-VIA = 5
+VIA = (3, 5, 7, 9)
 ALL = 64
 weights = (-205.0 / 72.0, 8.0 / 5.0, -1.0 / 5.0, 8.0 / 315.0, -1.0 / 560.0)
 
@@ -101,9 +101,16 @@
     for b in (at(1, 0), at(-1, 0), at(0, 1)):
         pl.semaphore_signal(barrier, inc=1, device_id={"band": b}, device_id_type=MESH)
 
-    @pl.loop(1, 16)
+    half = space // 8 * 8
+    turn = space - half
+
+    @pl.loop(1, 8)
     def _(k):
-        pl.semaphore_signal(barrier, inc=1, device_id={"space": lax.rem(space + k, 16)}, device_id_type=MESH)
+        pl.semaphore_signal(barrier, inc=1, device_id={"space": half + lax.rem(turn + k, 8)}, device_id_type=MESH)
+
+    opposite = lax.rem(space + 8, 16)
+    pl.semaphore_signal(barrier, inc=1, device_id={"space": opposite}, device_id_type=MESH)
+    pl.semaphore_signal(barrier, inc=1, device_id={"space": 15 - space}, device_id_type=MESH)
 
     local_copies = [
         pltpu.make_async_copy(blk.at[0], own3.at[pl.ds(0, 4), pl.ds(PAD, ROWS), :], loc_sem.at[0]),
@@ -113,7 +120,7 @@
     ]
     for copy in local_copies:
         copy.start()
-    pl.semaphore_wait(barrier, 18)
+    pl.semaphore_wait(barrier, 12)
 
     def source(part):
         return blk.at[part] if part < 2 else lat.at[pl.ds(4 * (part - 2), 4)]
@@ -127,15 +134,15 @@
 
     def detour(part, side):
         return pltpu.make_async_remote_copy(
-            src_ref=source(part), dst_ref=relay.at[part - VIA],
-            send_sem=halo_send.at[part, side], recv_sem=relay_recv.at[part - VIA],
+            src_ref=source(part), dst_ref=relay.at[VIA.index(part)],
+            send_sem=halo_send.at[part, side], recv_sem=relay_recv.at[VIA.index(part)],
             device_id={"space": space + 8 if side == 0 else space - 8}, device_id_type=MESH)
 
     def onward(part, side):
         ref = left3 if side == 0 else right3
         return pltpu.make_async_remote_copy(
-            src_ref=relay.at[part - VIA], dst_ref=ref.at[pl.ds(4 * part, 4), pl.ds(0, ROWS), :],
-            send_sem=relay_send.at[part - VIA], recv_sem=halo_recv.at[part, side],
+            src_ref=relay.at[VIA.index(part)], dst_ref=ref.at[pl.ds(4 * part, 4), pl.ds(0, ROWS), :],
+            send_sem=relay_send.at[VIA.index(part)], recv_sem=halo_recv.at[part, side],
             device_id={"space": space - 7 if side == 0 else space + 7}, device_id_type=MESH)
 
     senders = ((space < 15, space == 7, space != 7), (space > 0, space == 8, space != 8))
@@ -145,20 +152,20 @@
             @pl.when(any_)
             def _(side=side):
                 for part in parts:
-                    if part < VIA:
+                    if part not in VIA:
                         direct(part, side)
 
-            if any(part >= VIA for part in parts):
+            if set(VIA) & set(parts):
                 @pl.when(any_ & inner)
                 def _(side=side):
                     for part in parts:
-                        if part >= VIA:
+                        if part in VIA:
                             direct(part, side)
 
                 @pl.when(seam)
                 def _(side=side):
                     for part in parts:
-                        if part >= VIA:
+                        if part in VIA:
                             around(part, side)
 
     def halo_start(parts):
@@ -295,40 +302,37 @@
         arrived(t - 2)
         gram(t - 2)
 
-    gs[pl.ds(0, 96), :] = acc[:96] + acc[96:]
-    gs[pl.ds(96, 32), :] = jnp.zeros((32, 128), F32)
+    low64 = lanes((48, 128)) < 64
+    both = acc[:96] + acc[96:]
+    both = both + pltpu.roll(both, 64, 1)
+    gs[...] = jnp.where(low64, both[:48], both[48:])
 
     def scatter(k):
-        peer = lax.rem(space + k, 16)
         return pltpu.make_async_remote_copy(
-            src_ref=gs.at[pl.ds(8 * peer, 8), :], dst_ref=rbuf.at[space],
-            send_sem=rs_send.at[k], recv_sem=rs_recv.at[k], device_id={"space": peer}, device_id_type=MESH)
-
-    def spread(k):
-        peer = lax.rem(space + k, 16)
-        return pltpu.make_async_remote_copy(
-            src_ref=red, dst_ref=full.at[pl.ds(8 * space, 8), :],
-            send_sem=bc_send.at[k], recv_sem=bc_recv.at[k], device_id={"space": peer}, device_id_type=MESH)
-
-    for k in range(1, 16):
+            src_ref=gs, dst_ref=rbuf.at[turn], send_sem=rs_send.at[k], recv_sem=rs_recv.at[k],
+            device_id={"space": half + lax.rem(turn + k, 8)}, device_id_type=MESH)
+
+    cross = pltpu.make_async_remote_copy(
+        src_ref=red, dst_ref=full, send_sem=bc_send.at[0], recv_sem=bc_recv.at[0],
+        device_id={"space": opposite}, device_id_type=MESH)
+
+    for k in range(1, 8):
         scatter(k).start()
-    rbuf[pl.ds(space, 1)] = gs[pl.ds(8 * space, 8), :][None]
+    rbuf[pl.ds(turn, 1)] = gs[...][None]
     later(2)
     step(CHUNKS + 2)
-    for k in range(1, 16):
+    for k in range(1, 8):
         scatter(k).wait_recv()
     red[...] = jnp.sum(rbuf[...], axis=0)
-    for k in range(1, 16):
-        spread(k).start()
-    full[pl.ds(8 * space, 8), :] = red[...]
+    cross.start()
     later(3)
     step(CHUNKS + 3)
-    for k in range(1, 16):
-        spread(k).wait_recv()
+    cross.wait_recv()
 
     cells = 16.0 * ROWS * 128
-    total = full[...]
-    m1[...] = jnp.transpose(total + pltpu.roll(total, ALL, 1))[:ALL] * (1.0 / cells)
+    total = red[...] + full[...]
+    total = jnp.concatenate([total, pltpu.roll(total, 64, 1), jnp.zeros((32, 128), F32)], axis=0)
+    m1[...] = jnp.transpose(total)[:ALL] * (1.0 / cells)
     lane64 = lanes((ALL, 128))
     row64 = lax.broadcasted_iota(jnp.int32, (ALL, 128), 0)
     m2[...] = jnp.where((lane64 == row64) | (lane64 == row64 + ALL), 1.0, 0.0).astype(F32)
@@ -391,14 +395,28 @@
         outs[-1].start()
 
     halo_sent(range(10))
-    passed(range(VIA, 10))
+    passed(VIA)
     for u in range(UNITS):
         for sid in range(7):
             move(u, sid).wait_send()
-    for k in range(1, 16):
+    for k in range(1, 8):
         scatter(k).wait_send()
-        spread(k).wait_send()
+    cross.wait_send()
     for copy in outs:
+        copy.wait()
+
+
+def hand_over(hb, hl, hb_out, hl_out, held, get, put):
+    pairs = [(hb.at[i], hb_out.at[i]) for i in range(2)]
+    pairs += [(hl.at[pl.ds(4 * i, 4)], hl_out.at[pl.ds(4 * i, 4)]) for i in range(NL // 4)]
+    there = [pltpu.make_async_copy(src, held.at[i], get.at[i]) for i, (src, _) in enumerate(pairs)]
+    back = [pltpu.make_async_copy(held.at[i], dst, put.at[i]) for i, (_, dst) in enumerate(pairs)]
+    for copy in there:
+        copy.start()
+    for first, second in zip(there, back):
+        first.wait()
+        second.start()
+    for copy in back:
         copy.wait()
 
 
@@ -426,15 +444,15 @@
             pltpu.VMEM((41, PITCH, 128), F32),
             pltpu.VMEM((40, STEP, 128), F32),
             pltpu.VMEM((40, STEP, 128), F32),
-            pltpu.VMEM((10 - VIA, 4, ROWS, 128), F32),
+            pltpu.VMEM((len(VIA), 4, ROWS, 128), F32),
             pltpu.VMEM((2, 4, STEP, 128), F32),
             pltpu.VMEM((NL, STEP, 128), F32),
             pltpu.VMEM((2, 4, STEP, 128), F32),
             pltpu.VMEM((192, 128), F32),
-            pltpu.VMEM((128, 128), F32),
-            pltpu.VMEM((16, 8, 128), F32),
-            pltpu.VMEM((8, 128), F32),
-            pltpu.VMEM((128, 128), F32),
+            pltpu.VMEM((48, 128), F32),
+            pltpu.VMEM((8, 48, 128), F32),
+            pltpu.VMEM((48, 128), F32),
+            pltpu.VMEM((48, 128), F32),
             pltpu.VMEM((ALL, 128), F32),
             pltpu.VMEM((ALL, 128), F32),
             pltpu.VMEM((48, 256), BF16),
@@ -443,17 +461,27 @@
             pltpu.SemaphoreType.DMA((UNITS, 7)),
             pltpu.SemaphoreType.DMA((10, 2)),
             pltpu.SemaphoreType.DMA((10, 2)),
-            pltpu.SemaphoreType.DMA((10 - VIA,)),
-            pltpu.SemaphoreType.DMA((10 - VIA,)),
-            pltpu.SemaphoreType.DMA((16,)),
-            pltpu.SemaphoreType.DMA((16,)),
-            pltpu.SemaphoreType.DMA((16,)),
-            pltpu.SemaphoreType.DMA((16,)),
+            pltpu.SemaphoreType.DMA((len(VIA),)),
+            pltpu.SemaphoreType.DMA((len(VIA),)),
+            pltpu.SemaphoreType.DMA((8,)),
+            pltpu.SemaphoreType.DMA((8,)),
+            pltpu.SemaphoreType.DMA((1,)),
+            pltpu.SemaphoreType.DMA((1,)),
             pltpu.SemaphoreType.DMA((2, CHUNKS)),
         ],
         compiler_params=pltpu.CompilerParams(
             collective_id=0, has_side_effects=True, vmem_limit_bytes=56 * 1024 * 1024),
     )(rows_of(blocks), rows_of(later), rows_of(potential))
+    count = 2 + NL // 4
+    hb, hl = pl.pallas_call(
+        hand_over,
+        out_shape=[jax.ShapeDtypeStruct(hb.shape, F32), jax.ShapeDtypeStruct(hl.shape, F32)],
+        in_specs=[pl.BlockSpec(memory_space=pl.ANY)] * 2,
+        out_specs=[pl.BlockSpec(memory_space=pl.ANY)] * 2,
+        scratch_shapes=[pltpu.VMEM((count, 4, ROWS, 128), F32), pltpu.SemaphoreType.DMA((count,)),
+                        pltpu.SemaphoreType.DMA((count,))],
+        compiler_params=pltpu.CompilerParams(vmem_limit_bytes=56 * 1024 * 1024),
+    )(hb, hl)
     return planes_of(hb), planes_of(hl)
 
 

time: 129 us -> 121 us (0.938)
  local copies, waits for them, and re-layouts: 5.96 us -> 0 us
  Pallas kernels: 122 us -> 120 us
    unnamed x2 -> x0, local copies, waits for them, and re-layouts: 5.96 us -> none
    pallas_call x1, Pallas kernels: 122 us -> 117 us  [local(): pl.pallas_call(kernel, out_shape=[jax.ShapeDtypeStruct((2, 4, ROWS, 128),...]
    pallas_call x0 -> x1, Pallas kernels: none -> 3.41 us  [local(): pl.pallas_call(hand_over, out_shape=[jax.ShapeDtypeStruct(hb.shape, F32),...]
where the time goes in v4:
time: 121 us
  Pallas kernels  120 us (99%)
    pallas_call x1, Pallas kernels, local(): pl.pallas_call(kernel, out_shape=[jax.ShapeDtypeStruct((2, 4, ROWS, 128),...  117 us
    pallas_call x1, Pallas kernels, local(): pl.pallas_call(hand_over, out_shape=[jax.ShapeDtypeStruct(hb.shape, F32),...  3.41 us

profile of v4, /device:TPU:0, one launch (start us, length us, event | category | flops | bytes accessed | tf_op | source)
XLA Modules:
  0.0 120.6 jit_solution(17712978314061649659)
XLA Ops:
  0.6 116.5 %shard_map.50 = (f32[2,4,192,128]{3,2,1,0:T(8,128)}, f32[32,192,128]{2,1,0:T(8,128)}) custom-call(f32[2,4,192,128]{3,2,1,0:T(8,128)} %bitcast.26, f32[32,192,128]{2,1,0:T(8,128)} %bitcast.25, f32[192,128]{1,0:T(8,128)} %bitcast.27), custom_call_target="tpu_custom_call" | custom-call | tf_op jit(solution)/shard_map/pallas_call | solution.py:436
  117.2 3.4 %shard_map.51 = (f32[2,4,192,128]{3,2,1,0:T(8,128)}, f32[32,192,128]{2,1,0:T(8,128)}) custom-call(f32[2,4,192,128]{3,2,1,0:T(8,128)} %get-tuple-element.6.hb, f32[32,192,128]{2,1,0:T(8,128)} %get-tuple-element.7.hl), custom_call_target="tpu_custom_call" | custom-call | tf_op jit(solution)/shard_map/pallas_call | solution.py:476

commit v5 on v4

--- a/solution.py
+++ b/solution.py
@@ -221,11 +221,11 @@
             move(u, sid).start()
 
     def forward(u):
+        move(u, 0 if u % 2 == 0 else 1).wait_recv()
+        move(u, 3).start()
         move(u, 2).wait_recv()
         move(u, 4).start()
         move(u, 5).start()
-        move(u, 0 if u % 2 == 0 else 1).wait_recv()
-        move(u, 3).start()
 
     def across(u):
         move(u, 3).wait_recv()

time: 121 us -> 117 us (0.967)
  Pallas kernels: 120 us -> 116 us
    pallas_call x1, Pallas kernels: 117 us -> 113 us  [local(): pl.pallas_call(kernel, out_shape=[jax.ShapeDtypeStruct((2, 4, ROWS, 128),...]
where the time goes in v5:
time: 117 us
  Pallas kernels  116 us (99%)
    pallas_call x1, Pallas kernels, local(): pl.pallas_call(kernel, out_shape=[jax.ShapeDtypeStruct((2, 4, ROWS, 128),...  113 us
    pallas_call x1, Pallas kernels, local(): pl.pallas_call(hand_over, out_shape=[jax.ShapeDtypeStruct(hb.shape, F32),...  3.41 us

profile of v5, /device:TPU:0, one launch (start us, length us, event | category | flops | bytes accessed | tf_op | source)
XLA Modules:
  0.0 116.6 jit_solution(3224466338429882465)
XLA Ops:
  0.6 112.6 %shard_map.50 = (f32[2,4,192,128]{3,2,1,0:T(8,128)}, f32[32,192,128]{2,1,0:T(8,128)}) custom-call(f32[2,4,192,128]{3,2,1,0:T(8,128)} %bitcast.26, f32[32,192,128]{2,1,0:T(8,128)} %bitcast.25, f32[192,128]{1,0:T(8,128)} %bitcast.27), custom_call_target="tpu_custom_call" | custom-call | tf_op jit(solution)/shard_map/pallas_call | solution.py:436
  113.2 3.4 %shard_map.51 = (f32[2,4,192,128]{3,2,1,0:T(8,128)}, f32[32,192,128]{2,1,0:T(8,128)}) custom-call(f32[2,4,192,128]{3,2,1,0:T(8,128)} %get-tuple-element.6.hb, f32[32,192,128]{2,1,0:T(8,128)} %get-tuple-element.7.hl), custom_call_target="tpu_custom_call" | custom-call | tf_op jit(solution)/shard_map/pallas_call | solution.py:476

commit v6 on v5

--- a/solution.py
+++ b/solution.py
@@ -363,7 +363,7 @@
     coef = jnp.concatenate([mine, -proj[64:96], jnp.zeros((8, 128), F32)], axis=0)
     high = coef.astype(BF16).astype(F32)
     mixed = jnp.where(lanes((48, 128)) < 64, high, coef - high).astype(BF16)
-    lhs[...] = jnp.concatenate([mixed, mixed], axis=1)
+    lhs[...] = jnp.concatenate([mixed, mixed], axis=1)[:, :192]
     step(CHUNKS + 5)
     later(4)
     step(CHUNKS + 6)
@@ -377,7 +377,7 @@
             j4 = CROWS * c + 4 * step
             rows = jnp.concatenate([hmat[pl.ds(j4 + p, ALL, stride=STEP), :] for p in range(4)], axis=1)
             high, low = split(rows)
-            rhs = jnp.concatenate([high, high, low, low], axis=0)
+            rhs = jnp.concatenate([high, high, low], axis=0)
             res = jnp.dot(lhs[...], rhs, preferred_element_type=F32)
             for p in range(4):
                 piece = res[:, 128 * p:128 * p + 128]
@@ -455,7 +455,7 @@
             pltpu.VMEM((48, 128), F32),
             pltpu.VMEM((ALL, 128), F32),
             pltpu.VMEM((ALL, 128), F32),
-            pltpu.VMEM((48, 256), BF16),
+            pltpu.VMEM((48, 192), BF16),
             pltpu.SemaphoreType.DMA((5,)),
             pltpu.SemaphoreType.DMA((UNITS, 7)),
             pltpu.SemaphoreType.DMA((UNITS, 7)),

time: 117 us -> 117 us (level)
  no operation moved by 1% of the time
where the time goes in v6:
time: 117 us; the launch traced here: 116 us
  Pallas kernels  116 us (99%)
    pallas_call x1, Pallas kernels, local(): pl.pallas_call(kernel, out_shape=[jax.ShapeDtypeStruct((2, 4, ROWS, 128),...  112 us
    pallas_call x1, Pallas kernels, local(): pl.pallas_call(hand_over, out_shape=[jax.ShapeDtypeStruct(hb.shape, F32),...  3.41 us

profile of v6, /device:TPU:0, one launch (start us, length us, event | category | flops | bytes accessed | tf_op | source)
XLA Modules:
  0.0 116.2 jit_solution(1689038376762760757)
XLA Ops:
  0.6 112.2 %shard_map.50 = (f32[2,4,192,128]{3,2,1,0:T(8,128)}, f32[32,192,128]{2,1,0:T(8,128)}) custom-call(f32[2,4,192,128]{3,2,1,0:T(8,128)} %bitcast.26, f32[32,192,128]{2,1,0:T(8,128)} %bitcast.25, f32[192,128]{1,0:T(8,128)} %bitcast.27), custom_call_target="tpu_custom_call" | custom-call | tf_op jit(solution)/shard_map/pallas_call | solution.py:436
  112.8 3.4 %shard_map.51 = (f32[2,4,192,128]{3,2,1,0:T(8,128)}, f32[32,192,128]{2,1,0:T(8,128)}) custom-call(f32[2,4,192,128]{3,2,1,0:T(8,128)} %get-tuple-element.6.hb, f32[32,192,128]{2,1,0:T(8,128)} %get-tuple-element.7.hl), custom_call_target="tpu_custom_call" | custom-call | tf_op jit(solution)/shard_map/pallas_call | solution.py:476

commit v7 on v6

--- a/solution.py
+++ b/solution.py
@@ -274,6 +274,10 @@
         halo_wait((2 * g, 2 * g + 1))
         stencil(own, left, right, pot, g, (hacc, (g - 1) * (8 * STEP)))
 
+    def sent(u):
+        for sid in range(7):
+            move(u, sid).wait_send()
+
     def step(t):
         if t < UNITS:
             forward(t)
@@ -281,6 +285,8 @@
             across(t - 1)
         if t + 2 < UNITS:
             start_own(t + 2)
+        if t >= 4:
+            sent(t - 4)
         halo_start(HALOS.get(t, ()))
         pass_on(PASSES.get(t, ()))
 
@@ -396,9 +402,8 @@
 
     halo_sent(range(10))
     passed(VIA)
-    for u in range(UNITS):
-        for sid in range(7):
-            move(u, sid).wait_send()
+    for u in range(UNITS - 3, UNITS):
+        sent(u)
     for k in range(1, 8):
         scatter(k).wait_send()
     cross.wait_send()

time: 117 us -> 117 us (level)
  no operation moved by 1% of the time
where the time goes in v7:
time: 117 us; the launch traced here: 116 us
  Pallas kernels  116 us (99%)
    pallas_call x1, Pallas kernels, local(): pl.pallas_call(kernel, out_shape=[jax.ShapeDtypeStruct((2, 4, ROWS, 128),...  112 us
    pallas_call x1, Pallas kernels, local(): pl.pallas_call(hand_over, out_shape=[jax.ShapeDtypeStruct(hb.shape, F32),...  3.41 us

profile of v7, /device:TPU:0, one launch (start us, length us, event | category | flops | bytes accessed | tf_op | source)
XLA Modules:
  0.0 116.3 jit_solution(4402808558724923832)
XLA Ops:
  0.6 112.2 %shard_map.50 = (f32[2,4,192,128]{3,2,1,0:T(8,128)}, f32[32,192,128]{2,1,0:T(8,128)}) custom-call(f32[2,4,192,128]{3,2,1,0:T(8,128)} %bitcast.26, f32[32,192,128]{2,1,0:T(8,128)} %bitcast.25, f32[192,128]{1,0:T(8,128)} %bitcast.27), custom_call_target="tpu_custom_call" | custom-call | tf_op jit(solution)/shard_map/pallas_call | solution.py:441
  112.8 3.4 %shard_map.51 = (f32[2,4,192,128]{3,2,1,0:T(8,128)}, f32[32,192,128]{2,1,0:T(8,128)}) custom-call(f32[2,4,192,128]{3,2,1,0:T(8,128)} %get-tuple-element.6.hb, f32[32,192,128]{2,1,0:T(8,128)} %get-tuple-element.7.hl), custom_call_target="tpu_custom_call" | custom-call | tf_op jit(solution)/shard_map/pallas_call | solution.py:481
